TPU v7x, 32 devices: a whole 2x2x4 slice. The times are simulated.
32 devices in a mesh: doc: 4 (over z), feat: 8 (over y, x, core).
Axes of the slice: x: 2, y: 2, z: 4, core: 2. Of those that a mesh axis runs over, the one named last changes fastest.
Arguments:
- documents: bfloat16 [512, 512], P('doc', 'feat'), may hold values from -6 to 6
- directions: bfloat16 [512, 32768], P('doc', 'feat'), may hold values from -0.5 to 0.5
- phase: float32 [32768], P('feat'), may hold values from -3.140625 to 3.140625
- amplitude: float32 [32768], P('feat'), may hold values from 0.4 to 2.3
- doc_weight: float32 [512], P('doc'), may hold values from 0.5 to 4.2
- labels: int32 [512], P('doc'), may hold values from 0 to 127
Outputs:
- margins: float32 [512, 128], P('doc')
- scaled_weights: float32 [32768, 128], P('feat')
All inputs are finite; a program needn't handle non-finite values.
Results may differ from a plain program's by a relative error of at most 0.0003.
Values may be sent and summed in bfloat16 or wider, within the bound.
A program may use at most 64 MiB of HBM per device.

v0:
```python
import jax
import jax.numpy as jnp
from jax import lax
from jax.sharding import PartitionSpec as P

C = 128
ITERS = 3
NEWTON = 3
shrink_level = 0.1
ratio_floor = 1e-06


def project_tile(features, factor, start, target):
    residue = target - jnp.dot(features, start, precision=lax.Precision.HIGHEST)
    halfway = lax.linalg.triangular_solve(factor, residue, left_side=True, lower=True)
    solved = lax.linalg.triangular_solve(
        factor, halfway, left_side=True, lower=True, transpose_a=True
    )
    new_copy = start + lax.dot_general(
        features, solved, (((0,), (0,)), ((), ())), precision=lax.Precision.HIGHEST
    )
    new_part = jnp.dot(features, new_copy, precision=lax.Precision.HIGHEST)
    return (new_copy, new_part)


def logistic_prox(target, signs, weight_ratio):
    current = target
    for newton_step in range(NEWTON):
        chance = jax.nn.sigmoid(-signs * current)
        gradient = current - target - weight_ratio * signs * chance
        current = current - gradient / (1.0 + weight_ratio * chance * (1.0 - chance))
    return current


def shrink_values(target, limit):
    return target - jnp.clip(target, -limit, limit)


def per_device(documents, directions, phase, amplitude, doc_weight, labels):
    doc_full = lax.all_gather(documents, "feat", axis=1, tiled=True)
    doc_count = documents.shape[0]
    width_tile = directions.shape[1]
    num_feat = lax.axis_size("feat")
    num_doc = lax.axis_size("doc")
    angles = jnp.dot(
        doc_full,
        lax.all_gather(directions, "doc", axis=0, tiled=True),
        preferred_element_type=jnp.float32,
    )
    features = jnp.sqrt(2.0 / width_tile) * amplitude * jnp.cos(angles + phase)
    gram = jnp.eye(doc_count, dtype=jnp.float32) + lax.dot_general(
        features, features, (((1,), (1,)), ((), ())), precision=lax.Precision.HIGHEST
    )
    factor = jnp.linalg.cholesky(gram)
    signs = jnp.where(labels[:, None] == jnp.arange(C, dtype=jnp.int32)[None, :], 1.0, -1.0).astype(
        jnp.float32
    )
    share_rows = doc_count // num_feat
    offset = lax.axis_index("feat") * share_rows
    local_signs = lax.dynamic_slice_in_dim(signs, offset, share_rows, 0)
    local_weight = lax.dynamic_slice_in_dim(doc_weight, offset, share_rows, 0)[:, None]
    rho = jnp.float32(1.0)
    margins = logistic_prox(
        jnp.zeros(local_signs.shape, jnp.float32), local_signs, local_weight / rho
    )
    sums = jnp.zeros(local_signs.shape, jnp.float32)
    duals_y = jnp.zeros(local_signs.shape, jnp.float32)
    duals_x = jnp.zeros((width_tile, C), jnp.float32)
    partial_value = jnp.zeros((doc_count, C), jnp.float32)
    weights = jnp.zeros((width_tile, C), jnp.float32)
    for step in range(ITERS):
        correction = (margins - duals_y - sums) / num_feat
        correction = lax.all_gather(correction, "feat", axis=0, tiled=True)
        new_copy, partial_value = project_tile(
            features, factor, weights - duals_x, partial_value + correction
        )
        sums = lax.psum_scatter(partial_value, "feat", scatter_dimension=0, tiled=True)
        old_weights = weights
        old_margins = margins
        limit = shrink_level / (rho * num_doc)
        summed = lax.psum(new_copy + duals_x, "doc")
        weights = shrink_values(summed / num_doc, limit)
        margins = logistic_prox(sums + duals_y, local_signs, local_weight / rho)
        duals_x = duals_x + new_copy - weights
        duals_y = duals_y + sums - margins
        if step + 1 < ITERS:
            margin_gap = jnp.sum((sums - margins) ** 2)
            margin_move = jnp.sum((margins - old_margins) ** 2)
            primal, dual_norm = lax.psum(
                (
                    jnp.sum((new_copy - weights) ** 2) + margin_gap,
                    jnp.sum((weights - old_weights) ** 2) + margin_move,
                ),
                ("doc", "feat"),
            )
            dual_norm = rho * rho * dual_norm
            growth = ((primal + ratio_floor) / (dual_norm + ratio_floor)) ** 0.25
            rho = rho * growth
            duals_x = duals_x / growth
            duals_y = duals_y / growth
    margins = lax.all_gather(margins, "feat", axis=0, tiled=True)
    return (margins, num_feat * weights)


def solution(mesh):
    in_specs = (P("doc", "feat"), P("doc", "feat"), P("feat"), P("feat"), P("doc"), P("doc"))
    out_specs = (P("doc", None), P("feat", None))
    return jax.shard_map(
        per_device, mesh=mesh, in_specs=in_specs, out_specs=out_specs, check_vma=False
    )
```

profile of v0, /device:TPU:0, one launch (start us, length us, event | category | flops | bytes accessed | tf_op | source)
XLA Modules:
  0.0 668.8 jit_solution(7295771002411407596)
XLA Ops:
  9.6 10.7 %all_gather.20 = f32[128,128]{1,0:T(8,128)S(1)} all-gather(f32[16,128]{1,0:T(8,128)S(1)} %broadcast_multiply_fusion.1), channel_id=1, replica_groups=mesh['doc'=4,'feat'=8] {'feat'}, dimensions={0}, use_global_device_ids=true | all-gather | bytes 73728 | tf_op jit(solution)/shard_map/all_gather | solution.py:73
  20.3 9.2 %all_gather.18 = bf16[128,512]{0,1:T(8,128)(2,1)S(1)} all-gather(bf16[128,64]{0,1:T(8,128)(2,1)} %param.10), channel_id=1, replica_groups=mesh['doc'=4,'feat'=8] {'feat'}, dimensions={1}, use_global_device_ids=true | all-gather | bytes 147456 | tf_op jit(solution)/shard_map/all_gather | solution.py:40
  30.2 62.9 %all-gather.2.cloned.1.call-done = bf16[512,4096]{1,0:T(8,128)(2,1)} async-done(((bf16[128,4096]{1,0:T(8,128)(2,1)}), bf16[512,4096]{1,0:T(8,128)(2,1)}) %all-gather.2.cloned.1.call-update) | async-done | bytes 4194320 | tf_op jit(solution)/shard_map/all_gather | solution.py:47
  93.0 9.5 %fusion.1 = f32[128,4096]{1,0:T(8,128)S(1)} fusion(bf16[128,512]{0,1:T(8,128)(2,1)S(1)} %all_gather.18, bf16[512,4096]{1,0:T(8,128)(2,1)} %all-gather.2.cloned.1.call-done, f32[4096]{0:T(1024)} %param.12, f32[4096]{0:T(1024)S(1)} %broadcast_multiply_fusion), kind=kOutput, calls=%fused_computation.4 | convolution fusion | flops 537919488 | bytes 6455296 | tf_op jit(solution)/shard_map/dot_general | solution.py:45
  102.5 1.8 fusion.140
  104.3 1.8 convolution_subtract_fusion.2
  106.2 11.7 %cholesky.20 = f32[128,128]{1,0:T(8,128)S(1)} custom-call(f32[128,128]{1,0:T(8,128)S(1)} %fusion.22), custom_call_target="Cholesky" | custom-call | tf_op jit(solution)/shard_map/jit(cholesky)/cholesky | solution.py:54
  119.3 9.8 %custom-call.14 = f32[1,128,128]{1,2,0:T(8,128)S(1)} custom-call(f32[1,128,128]{2,1,0:T(8,128)S(1)} %fusion.8), custom_call_target="InvertDiagBlocksLowerTriangular" | custom-call | tf_op jit(solution)/shard_map/triangular_solve/custom-call.2 | solution.py:16
  129.6 16.5 %fusion.141 = f32[4096,128]{1,0:T(8,128)} fusion(f32[128,4096]{1,0:T(8,128)S(1)} %fusion.1, f32[128,128]{1,0:T(8,128)S(1)} %fusion.19), kind=kOutput, calls=%fused_computation.176 | convolution fusion | flops 805306368 | bytes 4259840 | tf_op jit(solution)/shard_map/dot_general | solution.py:19
  146.1 4.4 fusion.142
  151.2 31.4 %reduce-scatter.4.cloned.1.call-done = f32[16,128]{1,0:T(8,128)} async-done(((f32[128,128]{1,0:T(8,128)}), f32[16,128]{1,0:T(8,128)}) %reduce-scatter.4.cloned.1.call-update) | async-done | bytes 8208 | tf_op jit(solution)/shard_map/reduce_scatter | solution.py:77
  182.6 1.5 multiply_reduce_fusion.6
  185.5 86.3 %all-reduce.6.cloned.1.call-done = f32[4096,128]{1,0:T(8,128)} async-done(((f32[4096,128]{1,0:T(8,128)}), f32[4096,128]{1,0:T(8,128)}) %all-reduce.6.cloned.1.call-update) | async-done | bytes 2097168 | tf_op jit(solution)/shard_map/psum | solution.py:81
  271.8 3.4 multiply_reduce_fusion.2
  277.5 39.3 %all-reduce.1 = (f32[]{:T(128)}, f32[]{:T(128)}) all-reduce(f32[]{:T(128)S(6)} %add.189, f32[]{:T(128)S(6)} %add.191), channel_id=1, replica_groups=mesh['doc'=4,'feat'=8] {'doc','feat'}, use_global_device_ids=true, to_apply=%region_6.9 | all-reduce | flops 2 | bytes 16 | tf_op jit(solution)/shard_map/psum | solution.py:89
  318.2 10.2 %all_gather.21 = f32[128,128]{1,0:T(8,128)S(1)} all-gather(f32[16,128]{1,0:T(8,128)S(1)} %subtract_multiply_fusion.2), channel_id=1, replica_groups=mesh['doc'=4,'feat'=8] {'feat'}, dimensions={0}, use_global_device_ids=true | all-gather | bytes 73728 | tf_op jit(solution)/shard_map/all_gather | solution.py:73
  328.4 4.9 convolution_subtract_fusion.1
  333.8 5.1 fusion.5
  340.2 2.8 fusion.143
  343.8 31.9 %reduce-scatter.6.cloned.1.call-done = f32[16,128]{1,0:T(8,128)} async-done(((f32[128,128]{1,0:T(8,128)}), f32[16,128]{1,0:T(8,128)}) %reduce-scatter.6.cloned.1.call-update) | async-done | bytes 8208 | tf_op jit(solution)/shard_map/reduce_scatter | solution.py:77
  375.7 1.5 multiply_reduce_fusion.4
  377.2 87.4 %all-reduce.8.cloned.1.call-done = f32[4096,128]{1,0:T(8,128)} async-done(((f32[4096,128]{1,0:T(8,128)}), f32[4096,128]{1,0:T(8,128)}) %all-reduce.8.cloned.1.call-update) | async-done | bytes 2097168 | tf_op jit(solution)/shard_map/psum | solution.py:81
  464.7 4.4 multiply_reduce_fusion
  471.5 39.3 %all-reduce = (f32[]{:T(128)}, f32[]{:T(128)}) all-reduce(f32[]{:T(128)S(6)} %add.203, f32[]{:T(128)S(6)} %add.205), channel_id=1, replica_groups=mesh['doc'=4,'feat'=8] {'doc','feat'}, use_global_device_ids=true, to_apply=%region_14.17 | all-reduce | flops 2 | bytes 16 | tf_op jit(solution)/shard_map/psum | solution.py:89
  512.2 10.5 %all_gather.22 = f32[128,128]{1,0:T(8,128)S(1)} all-gather(f32[16,128]{1,0:T(8,128)S(1)} %subtract_multiply_fusion.1), channel_id=1, replica_groups=mesh['doc'=4,'feat'=8] {'feat'}, dimensions={0}, use_global_device_ids=true | all-gather | bytes 73728 | tf_op jit(solution)/shard_map/all_gather | solution.py:73
  522.7 5.0 convolution_subtract_fusion
  528.2 5.1 fusion.6
  533.3 2.8 fusion.144
  537.0 31.8 %reduce-scatter.8.cloned.1.call-done = f32[16,128]{1,0:T(8,128)} async-done(((f32[128,128]{1,0:T(8,128)}), f32[16,128]{1,0:T(8,128)}) %reduce-scatter.8.cloned.1.call-update) | async-done | bytes 8208 | tf_op jit(solution)/shard_map/reduce_scatter | solution.py:77
  569.6 9.2 %all_gather.23 = f32[128,128]{1,0:T(8,128)S(1)} all-gather(f32[16,128]{1,0:T(8,128)S(1)} %fusion.64), channel_id=1, replica_groups=mesh['doc'=4,'feat'=8] {'feat'}, dimensions={0}, use_global_device_ids=true | all-gather | bytes 73728 | tf_op jit(solution)/shard_map/all_gather | solution.py:101
  578.8 79.0 %all-reduce.10.cloned.1.call-done = f32[4096,128]{1,0:T(8,128)} async-done(((f32[4096,128]{1,0:T(8,128)}), f32[4096,128]{1,0:T(8,128)}) %all-reduce.10.cloned.1.call-update) | async-done | bytes 2097168 | tf_op jit(solution)/shard_map/psum | solution.py:81
  657.9 3.2 subtract_multiply_fusion
  (56 shorter events, 12.5 us)
Async XLA Ops:
  7.2 85.9 %all-gather.2.cloned.1.call-start = ((), (), s32[]{:S(2)}) async-start(), calls=%async_computation.3 | async-start | bytes 5242880 | tf_op jit(solution)/shard_map/all_gather | solution.py:47
  7.9 174.7 %reduce-scatter.4.cloned.1.call-start = ((), (), s32[]{:S(2)}) async-start(), calls=%async_computation.5 | async-start | bytes 73728 | tf_op jit(solution)/shard_map/reduce_scatter | solution.py:77
  150.5 121.3 %all-reduce.6.cloned.1.call-start = ((), (), s32[]{:S(2)}) async-start(), calls=%async_computation.4 | async-start | bytes 4194304 | tf_op jit(solution)/shard_map/psum | solution.py:81
  151.2 224.5 %reduce-scatter.6.cloned.1.call-start = ((), (), s32[]{:S(2)}) async-start(), calls=%async_computation.7 | async-start | bytes 73728 | tf_op jit(solution)/shard_map/reduce_scatter | solution.py:77
  185.5 132.7 %copy-start.8 = (f32[16,128]{1,0:T(8,128)S(1)}, f32[16,128]{1,0:T(8,128)}, u32[]{:S(2)}) copy-start(f32[16,128]{1,0:T(8,128)} %reduce-scatter.4.cloned.1.call-done) | copy-start | bytes 24580
  185.5 142.9 %copy-start.6 = (f32[128,128]{1,0:T(8,128)S(1)}, f32[128,128]{1,0:T(8,128)}, u32[]{:S(2)}) copy-start(f32[128,128]{1,0:T(8,128)} %fusion.142) | copy-start | bytes 196612
  328.4 5.4 copy-start
  328.4 5.4 copy-start.1
  338.9 1.3 copy-start.2
  343.0 0.7 copy-start.9
  343.0 121.6 %all-reduce.8.cloned.1.call-start = ((), (), s32[]{:S(2)}) async-start(), calls=%async_computation.6 | async-start | bytes 4194304 | tf_op jit(solution)/shard_map/psum | solution.py:81
  343.6 225.2 %reduce-scatter.8.cloned.1.call-start = ((), (), s32[]{:S(2)}) async-start(), calls=%async_computation.8 | async-start | bytes 73728 | tf_op jit(solution)/shard_map/reduce_scatter | solution.py:77
  377.2 135.0 %copy-start.7 = (f32[16,128]{1,0:T(8,128)S(1)}, f32[16,128]{1,0:T(8,128)}, u32[]{:S(2)}) copy-start(f32[16,128]{1,0:T(8,128)} %reduce-scatter.6.cloned.1.call-done) | copy-start | bytes 24580
  377.2 145.4 %copy-start.5 = (f32[128,128]{1,0:T(8,128)S(1)}, f32[128,128]{1,0:T(8,128)}, u32[]{:S(2)}) copy-start(f32[128,128]{1,0:T(8,128)} %fusion.143) | copy-start | bytes 196612
  522.7 5.5 copy-start.3
  522.7 5.5 copy-start.4
  536.1 121.8 %all-reduce.10.cloned.1.call-start = ((), (), s32[]{:S(2)}) async-start(), calls=%async_computation.9 | async-start | bytes 4194304 | tf_op jit(solution)/shard_map/psum | solution.py:81
Sparse Core Ops, SparseCore 0:
  9.5 83.4 all-gather.1
  150.6 32.0 reduce-scatter.3
  185.6 86.1 all-reduce.5
  343.2 32.5 reduce-scatter.5
  378.5 86.0 all-reduce.7
  536.2 32.5 reduce-scatter.7
  571.7 86.0 all-reduce.9
where the time goes:
time: 673 us; the launch traced here: 669 us
  waiting for transfers between devices  413 us (61%)
  blocking collectives  128 us (19%)
  matrix products  61 us (9%)
  other arithmetic  40.1 us (6%)
  between operations  22.2 us (3%)
    psum x3, waiting for transfers between devices, per_device(): summed = lax.psum(new_copy + duals_x, 'doc')  253 us
    reduce_scatter x3, waiting for transfers between devices, per_device(): lax.psum_scatter(partial_value, 'feat', scatter_dimension=0, tiled=True)  95.1 us
    psum x2, blocking collectives, per_device(): lax.psum((jnp.sum((new_copy - weights) ** 2) + margin_gap, jnp.sum((weigh...  78.6 us
    all_gather x1, waiting for transfers between devices, per_device(): lax.all_gather(directions, 'doc', axis=0, tiled=True)  62.9 us
    all_gather x3, blocking collectives, per_device(): correction = lax.all_gather(correction, 'feat', axis=0, tiled=True)  31.4 us
    dot_general x3, matrix products, project_tile(): lax.dot_general(features, solved, (((0,), (0,)), ((), ())), precision=lax...  26.6 us
  transfers between devices with their start and end apart: 7, of which 7 were waited for; matrix products, arithmetic and copies ran while one was open for 1% of the time, Pallas kernels for 0%

commit v1 on v0

--- a/solution.py
+++ b/solution.py
@@ -8,6 +8,24 @@
 NEWTON = 3
 shrink_level = 0.1
 ratio_floor = 1e-06
+
+
+def watch_task_over_axis(values):
+    axis_tag = "doc"
+    passed, upper, even = (lax.axis_size(axis_tag), lax.axis_index(axis_tag), values.shape[0])
+    next_value, part_next = (values, 1)
+    while part_next < passed:
+        chunks = []
+        at = 0
+        while at < passed:
+            chunks.append((at, (at - part_next) % passed))
+            at = at + 1
+        next_value = jnp.concatenate(
+            [next_value, lax.ppermute(next_value, axis_name=axis_tag, perm=chunks)], axis=0
+        )
+        part_next = 2 * part_next
+    tmp = jnp.roll(next_value, upper * even, axis=0)
+    return tmp
 
 
 def project_tile(features, factor, start, target):
@@ -42,11 +60,7 @@
     width_tile = directions.shape[1]
     num_feat = lax.axis_size("feat")
     num_doc = lax.axis_size("doc")
-    angles = jnp.dot(
-        doc_full,
-        lax.all_gather(directions, "doc", axis=0, tiled=True),
-        preferred_element_type=jnp.float32,
-    )
+    angles = jnp.dot(doc_full, watch_task_over_axis(directions), preferred_element_type=jnp.float32)
     features = jnp.sqrt(2.0 / width_tile) * amplitude * jnp.cos(angles + phase)
     gram = jnp.eye(doc_count, dtype=jnp.float32) + lax.dot_general(
         features, features, (((1,), (1,)), ((), ())), precision=lax.Precision.HIGHEST

time: 673 us -> 613 us (0.911)
  waiting for transfers between devices: 413 us -> 346 us
    psum x3, waiting for transfers between devices: 253 us -> 153 us  [per_device(): summed = lax.psum(new_copy + duals_x, 'doc')]
    ppermute x0 -> x2, waiting for transfers between devices: none -> 95.1 us  [watch_task_over_axis(): lax.ppermute(next_value, axis_name=axis_tag, perm=chunks)]
    all_gather x1 -> x0, waiting for transfers between devices: 62.9 us -> none  [per_device(): lax.all_gather(directions, 'doc', axis=0, tiled=True)]
    dot_general x3, matrix products: 26.6 us -> 10.1 us  [project_tile(): lax.dot_general(features, solved, (((0,), (0,)), ((), ())), precision=lax...]
  transfers between devices with their start and end apart: 7 -> 8, of which waited for: 7 -> 8; matrix products, arithmetic and copies ran while one was open for 1% -> 1% of each run, Pallas kernels for 0% -> 0%
where the time goes in v1:
time: 613 us; the launch traced here: 609 us
  waiting for transfers between devices  346 us (56%)
  blocking collectives  127 us (21%)
  matrix products  56.8 us (9%)
  other arithmetic  42.1 us (7%)
  between operations  23.8 us (4%)
  starting transfers between devices  6.75 us (1%)
    psum x3, waiting for transfers between devices, per_device(): summed = lax.psum(new_copy + duals_x, 'doc')  153 us
    reduce_scatter x3, waiting for transfers between devices, per_device(): lax.psum_scatter(partial_value, 'feat', scatter_dimension=0, tiled=True)  96.9 us
    ppermute x2, waiting for transfers between devices, watch_task_over_axis(): lax.ppermute(next_value, axis_name=axis_tag, perm=chunks)  95.1 us
    psum x2, blocking collectives, per_device(): lax.psum((jnp.sum((new_copy - weights) ** 2) + margin_gap, jnp.sum((weigh...  78.8 us
    all_gather x3, blocking collectives, per_device(): correction = lax.all_gather(correction, 'feat', axis=0, tiled=True)  30 us
    dot_general x3, matrix products, project_tile(): residue = target - jnp.dot(features, start, precision=lax.Precision.HIGHEST)  16 us
    dot_general x3, matrix products, project_tile(): new_part = jnp.dot(features, new_copy, precision=lax.Precision.HIGHEST)  13.9 us
    another operation x3, other arithmetic, per_device(): factor = jnp.linalg.cholesky(gram)  12.4 us
  transfers between devices with their start and end apart: 8, of which 8 were waited for; matrix products, arithmetic and copies ran while one was open for 1% of the time, Pallas kernels for 0%

profile of v1, /device:TPU:0, one launch (start us, length us, event | category | flops | bytes accessed | tf_op | source)
XLA Modules:
  0.0 609.1 jit_solution(15982903735560898293)
XLA Ops:
  8.1 5.1 collective-permute-start
  13.2 22.7 %collective-permute-done = bf16[128,4096]{1,0:T(8,128)(2,1)S(1)} collective-permute-done((bf16[128,4096]{1,0:T(8,128)(2,1)}, bf16[128,4096]{1,0:T(8,128)(2,1)S(1)}, u32[]{:S(2)}, u32[]{:S(2)}) %collective-permute-start) | collective-permute-done | bytes 1048608 | tf_op jit(solution)/shard_map/ppermute | solution.py:24
  40.4 9.3 %all_gather.16 = f32[128,128]{1,0:T(8,128)S(1)} all-gather(f32[16,128]{1,0:T(8,128)S(1)} %broadcast_multiply_fusion.1), channel_id=1, replica_groups=mesh['doc'=4,'feat'=8] {'feat'}, dimensions={0}, use_global_device_ids=true | all-gather | bytes 73728 | tf_op jit(solution)/shard_map/all_gather | solution.py:87
  49.6 9.2 %all_gather.15 = bf16[128,512]{0,1:T(8,128)(2,1)S(1)} all-gather(bf16[128,64]{0,1:T(8,128)(2,1)S(1)} %copy-done.11), channel_id=1, replica_groups=mesh['doc'=4,'feat'=8] {'feat'}, dimensions={1}, use_global_device_ids=true | all-gather | bytes 147456 | tf_op jit(solution)/shard_map/all_gather | solution.py:58
  59.0 72.4 %collective-permute-done.1 = bf16[256,4096]{1,0:T(8,128)(2,1)} collective-permute-done((bf16[256,4096]{1,0:T(8,128)(2,1)}, bf16[256,4096]{1,0:T(8,128)(2,1)}, u32[]{:S(2)}, u32[]{:S(2)}) %collective-permute-start.1) | collective-permute-done | bytes 2097184 | tf_op jit(solution)/shard_map/ppermute | solution.py:24
  135.0 11.8 %fusion.1 = f32[4096,128]{1,0:T(8,128)S(1)} fusion(bf16[128,512]{0,1:T(8,128)(2,1)S(1)} %all_gather.15, bf16[1024,4096]{1,0:T(8,128)(2,1)S(1)} %constant_dynamic-update-slice_fusion, s32[]{:T(128)S(6)} %select_n.26, f32[4096]{0:T(1024)S(1)} %copy-done.10, f32[4096]{0:T(1024)S(1)} %broadcast_multiply_fusion), kind=kOutput, calls=%fused_computation.4 | convolution fusion | flops 537919488 | bytes 6455300 | tf_op jit(solution)/shard_map/dot_general | solution.py:63
  146.9 3.5 fusion.142
  150.5 11.7 %cholesky.20 = f32[128,128]{1,0:T(8,128)S(1)} custom-call(f32[128,128]{1,0:T(8,128)S(1)} %fusion.23), custom_call_target="Cholesky" | custom-call | tf_op jit(solution)/shard_map/jit(cholesky)/cholesky | solution.py:68
  163.5 9.8 %custom-call.14 = f32[1,128,128]{1,2,0:T(8,128)S(1)} custom-call(f32[1,128,128]{2,1,0:T(8,128)S(1)} %fusion.9), custom_call_target="InvertDiagBlocksLowerTriangular" | custom-call | tf_op jit(solution)/shard_map/triangular_solve/custom-call.2 | solution.py:34
  173.3 3.6 convolution_subtract_fusion.2
  177.4 3.1 fusion.143
  180.5 5.7 fusion.144
  186.9 33.0 %reduce-scatter.4.cloned.1.call-done = f32[16,128]{1,0:T(8,128)} async-done(((f32[128,128]{1,0:T(8,128)}), f32[16,128]{1,0:T(8,128)}) %reduce-scatter.4.cloned.1.call-update) | async-done | bytes 8208 | tf_op jit(solution)/shard_map/reduce_scatter | solution.py:91
  222.6 53.0 %all-reduce.6.cloned.1.call-done = f32[4096,128]{1,0:T(8,128)} async-done(((f32[4096,128]{1,0:T(8,128)}), f32[4096,128]{1,0:T(8,128)}) %all-reduce.6.cloned.1.call-update) | async-done | bytes 2097168 | tf_op jit(solution)/shard_map/psum | solution.py:95
  275.6 3.4 multiply_reduce_fusion.2
  281.4 39.3 %all-reduce.1 = (f32[]{:T(128)}, f32[]{:T(128)}) all-reduce(f32[]{:T(128)S(6)} %add.202, f32[]{:T(128)S(6)} %add.204), channel_id=1, replica_groups=mesh['doc'=4,'feat'=8] {'doc','feat'}, use_global_device_ids=true, to_apply=%region_6.9 | all-reduce | flops 2 | bytes 16 | tf_op jit(solution)/shard_map/psum | solution.py:103
  322.0 10.4 %all_gather.17 = f32[128,128]{1,0:T(8,128)S(1)} all-gather(f32[16,128]{1,0:T(8,128)S(1)} %subtract_multiply_fusion.2), channel_id=1, replica_groups=mesh['doc'=4,'feat'=8] {'feat'}, dimensions={0}, use_global_device_ids=true | all-gather | bytes 73728 | tf_op jit(solution)/shard_map/all_gather | solution.py:87
  332.5 6.2 %convolution_subtract_fusion.1 = f32[128,128]{1,0:T(8,128)S(1)} fusion(f32[4096,128]{1,0:T(8,128)S(1)} %fusion.1, f32[128,128]{1,0:T(8,128)S(1)} %copy-done.7, f32[128,128]{1,0:T(8,128)S(1)} %all_gather.17, f32[4096,128]{1,0:T(8,128)} %all-reduce.6.cloned.1.call-done, f32[]{:T(128)S(6)} %pow.6, f32[4096,128]{1,0:T(8,128)} %fusion.143), kind=kOutput, calls=%fused_computation.16 | convolution fusion | flops 808484864 | bytes 6488068 | tf_op jit(solution)/shard_map/dot_general | solution.py:32
  339.2 3.5 fusion.6
  344.0 4.1 fusion.145
  348.9 31.9 %reduce-scatter.6.cloned.1.call-done = f32[16,128]{1,0:T(8,128)} async-done(((f32[128,128]{1,0:T(8,128)}), f32[16,128]{1,0:T(8,128)}) %reduce-scatter.6.cloned.1.call-update) | async-done | bytes 8208 | tf_op jit(solution)/shard_map/reduce_scatter | solution.py:91
  382.3 54.2 %all-reduce.8.cloned.1.call-done = f32[4096,128]{1,0:T(8,128)} async-done(((f32[4096,128]{1,0:T(8,128)}), f32[4096,128]{1,0:T(8,128)}) %all-reduce.8.cloned.1.call-update) | async-done | bytes 2097168 | tf_op jit(solution)/shard_map/psum | solution.py:95
  436.5 4.4 multiply_reduce_fusion
  443.4 39.5 %all-reduce = (f32[]{:T(128)}, f32[]{:T(128)}) all-reduce(f32[]{:T(128)S(6)} %add.216, f32[]{:T(128)S(6)} %add.218), channel_id=1, replica_groups=mesh['doc'=4,'feat'=8] {'doc','feat'}, use_global_device_ids=true, to_apply=%region_14.17 | all-reduce | flops 2 | bytes 16 | tf_op jit(solution)/shard_map/psum | solution.py:103
  484.3 10.3 %all_gather.18 = f32[128,128]{1,0:T(8,128)S(1)} all-gather(f32[16,128]{1,0:T(8,128)S(1)} %subtract_multiply_fusion.1), channel_id=1, replica_groups=mesh['doc'=4,'feat'=8] {'feat'}, dimensions={0}, use_global_device_ids=true | all-gather | bytes 73728 | tf_op jit(solution)/shard_map/all_gather | solution.py:87
  494.6 6.2 %convolution_subtract_fusion = f32[128,128]{1,0:T(8,128)S(1)} fusion(f32[4096,128]{1,0:T(8,128)S(1)} %fusion.1, f32[128,128]{1,0:T(8,128)S(1)} %copy-done.6, f32[128,128]{1,0:T(8,128)S(1)} %all_gather.18, f32[]{:T(128)S(6)} %pow.7, f32[4096,128]{1,0:T(8,128)} %get-tuple-element.19, f32[]{:T(128)S(6)} %neg.63, f32[]{:T(128)S(6)} %div.173, ...), kind=kOutput, calls=%fused_computation.15 | convolution fusion | flops 809009152 | bytes 6488076 | tf_op jit(solution)/shard_map/dot_general | solution.py:32
  501.4 3.5 fusion.7
  504.9 4.1 fusion.146
  509.7 32.0 %reduce-scatter.8.cloned.1.call-done = f32[16,128]{1,0:T(8,128)} async-done(((f32[128,128]{1,0:T(8,128)}), f32[16,128]{1,0:T(8,128)}) %reduce-scatter.8.cloned.1.call-update) | async-done | bytes 8208 | tf_op jit(solution)/shard_map/reduce_scatter | solution.py:91
  542.6 9.2 %all_gather.19 = f32[128,128]{1,0:T(8,128)S(1)} all-gather(f32[16,128]{1,0:T(8,128)S(1)} %fusion.65), channel_id=1, replica_groups=mesh['doc'=4,'feat'=8] {'feat'}, dimensions={0}, use_global_device_ids=true | all-gather | bytes 73728 | tf_op jit(solution)/shard_map/all_gather | solution.py:115
  551.8 45.7 %all-reduce.10.cloned.1.call-done = f32[4096,128]{1,0:T(8,128)} async-done(((f32[4096,128]{1,0:T(8,128)}), f32[4096,128]{1,0:T(8,128)}) %all-reduce.10.cloned.1.call-update) | async-done | bytes 2097168 | tf_op jit(solution)/shard_map/psum | solution.py:95
  597.4 3.2 subtract_multiply_fusion
  (74 shorter events, 20.2 us)
Async XLA Ops:
  8.0 50.8 %copy-start.3 = (bf16[128,4096]{1,0:T(8,128)(2,1)S(1)}, bf16[128,4096]{1,0:T(8,128)(2,1)}, u32[]{:S(2)}) copy-start(bf16[128,4096]{1,0:T(8,128)(2,1)} %param.11) | copy-start | bytes 3145732
  8.0 32.1 %copy-start.14 = (s32[128]{0:T(128)S(1)}, s32[128]{0:T(128)}, u32[]{:S(2)}) copy-start(s32[128]{0:T(128)} %param.15) | copy-start | bytes 1540
  8.0 32.1 %copy-start.13 = (f32[128]{0:T(128)S(1)}, f32[128]{0:T(128)}, u32[]{:S(2)}) copy-start(f32[128]{0:T(128)} %param.14) | copy-start | bytes 1540
  8.0 41.6 %copy-start.11 = (bf16[128,64]{0,1:T(8,128)(2,1)S(1)}, bf16[128,64]{0,1:T(8,128)(2,1)}, u32[]{:S(2)}) copy-start(bf16[128,64]{0,1:T(8,128)(2,1)} %param.10) | copy-start | bytes 49156
  8.0 50.8 %copy-start.12 = (f32[4096]{0:T(1024)S(1)}, f32[4096]{0:T(1024)}, u32[]{:S(2)}) copy-start(f32[4096]{0:T(1024)} %param.13) | copy-start | bytes 49156
  8.0 211.8 %reduce-scatter.4.cloned.1.call-start = ((), (), s32[]{:S(2)}) async-start(), calls=%async_computation.4 | async-start | bytes 73728 | tf_op jit(solution)/shard_map/reduce_scatter | solution.py:91
  8.1 27.9 %collective-permute-start = (bf16[128,4096]{1,0:T(8,128)(2,1)}, bf16[128,4096]{1,0:T(8,128)(2,1)S(1)}, u32[]{:S(2)}, u32[]{:S(2)}) collective-permute-start(bf16[128,4096]{1,0:T(8,128)(2,1)} %param.11), channel_id=1, source_target_pairs={{0,24},{8,0},{16,8},{24,16},{1,25},{9,1},{17,9},{25,17},{2,26},{10... | collective-permute-start | bytes 3145736 | tf_op jit(solution)/shard_map/ppermute | solution.py:24
  38.7 92.7 %collective-permute-start.1 = (bf16[256,4096]{1,0:T(8,128)(2,1)}, bf16[256,4096]{1,0:T(8,128)(2,1)}, u32[]{:S(2)}, u32[]{:S(2)}) collective-permute-start(bf16[256,4096]{1,0:T(8,128)(2,1)} %pad_maximum_fusion), channel_id=1, source_target_pairs={{0,16},{8,24},{16,0},{24,8},{1,17},{9,25},{17,1},{25,9},{2,18},{10... | collective-permute-start | bytes 6291464 | tf_op jit(solution)/shard_map/ppermute | solution.py:24
  133.3 1.8 copy-start.10
  186.2 89.3 %all-reduce.6.cloned.1.call-start = ((), (), s32[]{:S(2)}) async-start(), calls=%async_computation.3 | async-start | bytes 4194304 | tf_op jit(solution)/shard_map/psum | solution.py:95
  186.8 194.0 %reduce-scatter.6.cloned.1.call-start = ((), (), s32[]{:S(2)}) async-start(), calls=%async_computation.6 | async-start | bytes 73728 | tf_op jit(solution)/shard_map/reduce_scatter | solution.py:91
  222.6 99.4 %copy-start.9 = (f32[16,128]{1,0:T(8,128)S(1)}, f32[16,128]{1,0:T(8,128)}, u32[]{:S(2)}) copy-start(f32[16,128]{1,0:T(8,128)} %reduce-scatter.4.cloned.1.call-done) | copy-start | bytes 24580
  222.6 109.9 %copy-start.7 = (f32[128,128]{1,0:T(8,128)S(1)}, f32[128,128]{1,0:T(8,128)}, u32[]{:S(2)}) copy-start(f32[128,128]{1,0:T(8,128)} %fusion.144) | copy-start | bytes 196612
  332.5 6.7 %copy-start = (f32[4096,128]{1,0:T(8,128)S(1)}, f32[4096,128]{1,0:T(8,128)}, u32[]{:S(2)}) copy-start(f32[4096,128]{1,0:T(8,128)} %fusion.143) | copy-start | bytes 6291460
  332.5 6.7 %copy-start.1 = (f32[4096,128]{1,0:T(8,128)S(1)}, f32[4096,128]{1,0:T(8,128)}, u32[]{:S(2)}) copy-start(f32[4096,128]{1,0:T(8,128)} %all-reduce.6.cloned.1.call-done) | copy-start | bytes 6291460
  342.6 1.3 copy-start.2
  348.1 88.4 %all-reduce.8.cloned.1.call-start = ((), (), s32[]{:S(2)}) async-start(), calls=%async_computation.5 | async-start | bytes 4194304 | tf_op jit(solution)/shard_map/psum | solution.py:95
  348.7 193.0 %reduce-scatter.8.cloned.1.call-start = ((), (), s32[]{:S(2)}) async-start(), calls=%async_computation.7 | async-start | bytes 73728 | tf_op jit(solution)/shard_map/reduce_scatter | solution.py:91
  382.3 102.0 %copy-start.8 = (f32[16,128]{1,0:T(8,128)S(1)}, f32[16,128]{1,0:T(8,128)}, u32[]{:S(2)}) copy-start(f32[16,128]{1,0:T(8,128)} %reduce-scatter.6.cloned.1.call-done) | copy-start | bytes 24580
  382.3 112.3 %copy-start.6 = (f32[128,128]{1,0:T(8,128)S(1)}, f32[128,128]{1,0:T(8,128)}, u32[]{:S(2)}) copy-start(f32[128,128]{1,0:T(8,128)} %fusion.145) | copy-start | bytes 196612
  494.6 6.8 %copy-start.4 = (f32[4096,128]{1,0:T(8,128)S(1)}, f32[4096,128]{1,0:T(8,128)}, u32[]{:S(2)}) copy-start(f32[4096,128]{1,0:T(8,128)} %get-tuple-element.19) | copy-start | bytes 6291460
  494.6 6.8 %copy-start.5 = (f32[4096,128]{1,0:T(8,128)S(1)}, f32[4096,128]{1,0:T(8,128)}, u32[]{:S(2)}) copy-start(f32[4096,128]{1,0:T(8,128)} %all-reduce.8.cloned.1.call-done) | copy-start | bytes 6291460
  509.0 88.4 %all-reduce.10.cloned.1.call-start = ((), (), s32[]{:S(2)}) async-start(), calls=%async_computation.8 | async-start | bytes 4194304 | tf_op jit(solution)/shard_map/psum | solution.py:95
Sparse Core Ops, SparseCore 0:
  186.4 33.4 reduce-scatter.3
  348.2 32.5 reduce-scatter.5
  509.2 32.5 reduce-scatter.7
Sparse Core Ops, SparseCore 1:
  189.7 85.8 all-reduce.5
  351.5 84.9 all-reduce.7
  512.4 84.9 all-reduce.9
